TPU v7x, 512 devices: a whole 4x8x8 slice. The times are simulated.
512 devices in a mesh: nest: 8 (over x, z_hi), gx: 8 (over y), gy: 8 (over z_lo, core).
Axes of the slice: x: 4, y: 8, z: 8 (z_hi: 2, z_lo: 4; z = z_hi * 4 + z_lo), core: 2. Of those that a mesh axis runs over, the one named last changes fastest.
Arguments:
- state: float32 [8, 4, 8, 128, 1024], P('nest', None, None, 'gx', 'gy'), may hold values from -6 to 6
- metric: float32 [8, 3, 128, 1024], P('nest', None, 'gx', 'gy'), may hold values from -1.2 to 1.4, as said below
- placement: int32 [7, 2], replicated, may hold values from 0 to 682, as said below
- zones: int32 [7, 4], replicated, may hold values from 2 to 5
Outputs:
- new_state: float32 [8, 4, 8, 128, 1024], P('nest', None, None, 'gx', 'gy')
Inputs may be any that keep to these rules, and one draw needn't show every extreme that they name: metric[:, 0] and metric[:, 1] are terrain slopes; metric[:, 2] is the column stretch, between 0.6 and 1.4. placement[n] = (ox, oy) with ox <= 85 and oy <= 682.
All inputs are finite; a program needn't handle non-finite values.
Results may differ from a plain program's by a relative error of at most 0.0003.
Values sent between devices are 32-bit elements; how exact they have to be, the bound alone decides.
No kernel may reach another device: no remote copies, remote signals or barrier semaphores. Data moves between devices by JAX's collectives and lax.ppermute only.
A program may use at most 64 MiB of HBM per device.

v0:
```python
import jax
import jax.numpy as jnp
from jax import lax
from jax.sharding import PartitionSpec as P

SUB = 4
R = 3
W_MAX = 5
WP = 3
TIME_STEP = 0.5
SOUND_SQ = 1.0
PRECISE = lax.Precision.HIGHEST


def extended(value, sides, width):
    for axis, dim in sides:
        devices, length = (lax.axis_size(axis), value.shape[dim])
        up = [(i, (i + 1) % devices) for i in range(devices - 1)]
        down = [(j, i) for i, j in up]
        last = lax.slice_in_dim(value, length - width, length, axis=dim)
        initial = lax.slice_in_dim(value, 0, width, axis=dim)
        before = lax.ppermute(last, axis, up)
        after = lax.ppermute(initial, axis, down)
        value = jnp.concatenate([before, value, after], axis=dim)
    return value


def broadcast(block, axis, owner):
    block = jnp.where(lax.axis_index(axis) == owner, block, jnp.zeros_like(block))
    return lax.psum(block, axis)


def vertical(field):
    upper = jnp.concatenate([field[1:], field[-1:]], 0)
    lower = jnp.concatenate([field[:1], field[:-1]], 0)
    return (upper - lower) * 0.5


def edge_weight(zone_width, row_index, col_index, total_x, total_y):
    widths = zone_width.astype(jnp.float32)
    row_pos = row_index.astype(jnp.float32)[:, None]
    col_pos = col_index.astype(jnp.float32)[None, :]
    dists = (row_pos, total_x - 1 - row_pos, col_pos, total_y - 1 - col_pos)
    weight = jnp.zeros((row_index.shape[0], col_index.shape[0]), jnp.float32)
    for edge in range(4):
        weight = jnp.maximum(weight, jnp.maximum((widths[edge] - dists[edge]) / widths[edge], 0.0))
    return weight


def step_each(current, terrain, sigma_col):
    wind_x, wind_y, updraft, pressure = current
    pressure_ext = extended(pressure, (("gx", 1), ("gy", 2)), 1)
    press_z = vertical(pressure) / terrain[2]
    grad_x = (pressure_ext[:, 2:, 1:-1] - pressure_ext[:, :-2, 1:-1]) * 0.5
    grad_y = (pressure_ext[:, 1:-1, 2:] - pressure_ext[:, 1:-1, :-2]) * 0.5
    new_x = wind_x - TIME_STEP * (grad_x - sigma_col * terrain[0] * press_z)
    new_y = wind_y - TIME_STEP * (grad_y - sigma_col * terrain[1] * press_z)
    new_w = updraft - TIME_STEP * press_z
    winds_ext = extended(jnp.stack([new_x, new_y]), (("gx", 2), ("gy", 3)), 1)
    spread = (winds_ext[0, :, 2:, 1:-1] - winds_ext[0, :, :-2, 1:-1]) * 0.5 + (
        winds_ext[1, :, 1:-1, 2:] - winds_ext[1, :, 1:-1, :-2]
    ) * 0.5
    spread = (
        spread
        - sigma_col * (terrain[0] * vertical(new_x) + terrain[1] * vertical(new_y)) / terrain[2]
        + vertical(new_w) / terrain[2]
    )
    return (new_x, new_y, new_w, pressure - TIME_STEP * SOUND_SQ * spread)


def boundary_pieces(
    parent_tile, placement, row_start, col_start, total_x, total_y, foot_x, foot_y, span_len
):
    row_index = row_start + jnp.arange(parent_tile.shape[2], dtype=jnp.int32)
    col_index = col_start + jnp.arange(parent_tile.shape[3], dtype=jnp.int32)
    depth_range = jnp.arange(WP, dtype=jnp.int32)
    reach_range = jnp.arange(span_len, dtype=jnp.int32)
    west_x = placement[:, 0:1]
    south_y = placement[:, 1:2]
    east_base = (total_x - 1) // R - (WP - 1)
    north_base = (total_y - 1) // R - (WP - 1)
    x_depth = jnp.stack([west_x + depth_range, west_x + east_base + depth_range], 1)
    y_depth = jnp.stack([south_y + depth_range, south_y + north_base + depth_range], 1)
    x_reach = jnp.where(reach_range < foot_x, west_x + reach_range, -1)
    y_reach = jnp.where(reach_range < foot_y, south_y + reach_range, -1)
    pick_rows = (x_depth[..., None] == row_index).astype(jnp.float32)
    pick_cols = (y_reach[:, None, :] == col_index[None, :, None]).astype(jnp.float32)
    across = jnp.einsum("neai,flij->neflaj", pick_rows, parent_tile, precision=PRECISE)
    across = jnp.einsum("neflaj,njb->neflab", across, pick_cols, precision=PRECISE)
    pick_depth = (y_depth[..., None] == col_index).astype(jnp.float32)
    pick_reach = (x_reach[:, None, :] == row_index[None, :, None]).astype(jnp.float32)
    along_y = jnp.einsum("neaj,flij->neflai", pick_depth, parent_tile, precision=PRECISE)
    along_y = jnp.einsum("neflai,nib->neflab", along_y, pick_reach, precision=PRECISE)
    return jnp.concatenate([across, along_y], 1)


def relax_edges(relaxed_in, own_pieces, zone_width, row_start, col_start, total_x, total_y, active):
    row_index = row_start + jnp.arange(relaxed_in.shape[2], dtype=jnp.int32)
    col_index = col_start + jnp.arange(relaxed_in.shape[3], dtype=jnp.int32)
    depth_range = jnp.arange(WP, dtype=jnp.int32)
    reach_range = jnp.arange(own_pieces.shape[-1], dtype=jnp.int32)
    east_base = (total_x - 1) // R - (WP - 1)
    north_base = (total_y - 1) // R - (WP - 1)
    west_pick = ((row_index < W_MAX)[:, None] & ((row_index // R)[:, None] == depth_range)).astype(
        jnp.float32
    )
    east_pick = (
        (row_index >= total_x - W_MAX)[:, None]
        & ((row_index // R - east_base)[:, None] == depth_range)
    ).astype(jnp.float32)
    south_pick = ((col_index < W_MAX)[:, None] & ((col_index // R)[:, None] == depth_range)).astype(
        jnp.float32
    )
    north_pick = (
        (col_index >= total_y - W_MAX)[:, None]
        & ((col_index // R - north_base)[:, None] == depth_range)
    ).astype(jnp.float32)
    col_reach = (reach_range[:, None] == (col_index // R)[None, :]).astype(jnp.float32)
    row_reach = (reach_range[:, None] == (row_index // R)[None, :]).astype(jnp.float32)
    across = jnp.einsum("eflab,bj->eflaj", own_pieces[0:2], col_reach, precision=PRECISE)
    from_x = jnp.einsum("ia,flaj->flij", west_pick, across[0], precision=PRECISE) + jnp.einsum(
        "ia,flaj->flij", east_pick, across[1], precision=PRECISE
    )
    along_y = jnp.einsum("eflab,bi->eflai", own_pieces[2:4], row_reach, precision=PRECISE)
    from_y = jnp.einsum("ja,flai->flij", south_pick, along_y[0], precision=PRECISE) + jnp.einsum(
        "ja,flai->flij", north_pick, along_y[1], precision=PRECISE
    )
    in_x = (row_index < W_MAX) | (row_index >= total_x - W_MAX)
    target = jnp.where(in_x[:, None], from_x, from_y)
    weight = edge_weight(zone_width, row_index, col_index, total_x, total_y)
    weight = jnp.where(active, weight, 0.0)
    return relaxed_in + weight * (target - relaxed_in)


def local(state, metric, placement, zones):
    fields = state[0]
    terrain = metric[0]
    levels, size_x, size_y = (fields.shape[1], fields.shape[2], fields.shape[3])
    total_x = size_x * lax.axis_size("gx")
    total_y = size_y * lax.axis_size("gy")
    nest_count = placement.shape[0]
    group_index = lax.axis_index("nest")
    row_start = lax.axis_index("gx") * size_x
    col_start = lax.axis_index("gy") * size_y
    foot_x = (total_x + R - 1) // R
    foot_y = (total_y + R - 1) // R
    span_len = 64 * ((max(foot_x, foot_y) + 63) // 64)
    own_group = jnp.minimum(group_index, nest_count - 1)
    start_three = jnp.stack([fields[0], fields[1], fields[3]])
    pieces = boundary_pieces(
        start_three, placement, row_start, col_start, total_x, total_y, foot_x, foot_y, span_len
    )
    summed = lax.psum(pieces, ("gx", "gy"))
    arrived = broadcast(summed, "nest", nest_count)
    own_pieces = arrived[own_group]
    sigma_col = (1.0 - (jnp.arange(levels, dtype=jnp.float32) + 0.5) / levels)[:, None, None]
    current = (fields[0], fields[1], fields[2], fields[3])
    for substep in range(SUB):
        current = step_each(current, terrain, sigma_col)
    active = group_index < nest_count
    moved_three = jnp.stack([current[0], current[1], current[3]])
    relaxed = relax_edges(
        moved_three, own_pieces, zones[own_group], row_start, col_start, total_x, total_y, active
    )
    result = jnp.stack([relaxed[0], relaxed[1], current[2], relaxed[2]])
    return result[None]


def solution(mesh):
    return jax.shard_map(
        local,
        mesh=mesh,
        in_specs=(P("nest", None, None, "gx", "gy"), P("nest", None, "gx", "gy"), P(), P()),
        out_specs=P("nest", None, None, "gx", "gy"),
        check_vma=False,
    )
```

profile of v0, /device:TPU:1, one launch (start us, length us, event | category | flops | bytes accessed | tf_op | source)
XLA Modules:
  0.0 865.6 jit_solution(14164995903394578647)
XLA Ops:
  11.9 1.9 pad_maximum_fusion
  13.9 4.2 collective-permute-start.1
  23.2 5.4 collective-permute-start.3
  28.5 2.5 collective-permute-start.2
  31.2 3.3 collective-permute-done.2
  36.0 4.4 collective-permute-start.5
  41.3 2.7 collective-permute-start.7
  46.7 5.1 collective-permute-done.6
  52.0 3.6 collective-permute-start.9
  57.0 5.0 collective-permute-done.8
  62.1 2.5 collective-permute-start.11
  66.7 3.9 collective-permute-done.10
  72.1 5.1 collective-permute-start.13
  78.1 2.7 collective-permute-start.15
  83.4 4.7 collective-permute-done.14
  88.3 6.4 collective-permute-start.17
  96.0 3.9 collective-permute-done.16
  100.1 2.1 collective-permute-start.19
  102.2 2.2 collective-permute-start.18
  104.5 4.1 collective-permute-done.18
  110.1 4.9 collective-permute-start.21
  115.9 2.7 collective-permute-start.23
  121.5 6.1 collective-permute-done.22
  127.8 4.3 collective-permute-start.25
  133.5 438.1 %all-reduce.3.cloned.1.call-done = f32[7,4,3,8,3,384]{5,3,4,2,1,0:T(8,128)} async-done(((f32[7,4,3,8,3,384]{5,3,4,2,1,0:T(8,128)}), f32[7,4,3,8,3,384]{5,3,4,2,1,0:T(8,128)}) %all-reduce.3.cloned.1.call-update) | async-done | bytes 3096592 | tf_op jit(solution)/shard_map/psum | solution.py:153
  575.6 3.8 collective-permute-start.26
  579.4 2.1 collective-permute-done.26
  583.0 4.0 collective-permute-start.29
  588.0 3.0 collective-permute-start.31
  592.9 5.6 collective-permute-done.31
  598.5 62.3 %collective-permute-done.30 = f32[2,8,18,1]{3,2,1,0:T(8,128)S(1)} collective-permute-done((f32[2,8,18,1]{3,2,1,0:T(8,128)S(1)}, f32[2,8,18,1]{3,2,1,0:T(8,128)S(1)}, u32[]{:S(2)}, u32[]{:S(2)}) %collective-permute-start.30) | collective-permute-done | bytes 1184 | tf_op jit(solution)/shard_map/ppermute | solution.py:23
  661.1 193.1 %all-reduce.5.cloned.1.call-done = f32[7,4,3,8,3,384]{5,3,4,2,1,0:T(8,128)} async-done(((f32[7,4,3,8,3,384]{5,3,4,2,1,0:T(8,128)}), f32[7,4,3,8,3,384]{5,3,4,2,1,0:T(8,128)}) %all-reduce.5.cloned.1.call-update) | async-done | bytes 3096592 | tf_op jit(solution)/shard_map/psum | solution.py:30
  (159 shorter events, 45.6 us)
Async XLA Ops:
  6.5 565.0 %all-reduce.3.cloned.1.call-start = ((), (), s32[]{:S(2)}) async-start(), calls=%async_computation | async-start | bytes 6193152 | tf_op jit(solution)/shard_map/psum | solution.py:153
  13.8 840.3 %all-reduce.5.cloned.1.call-start = ((), (), s32[]{:S(2)}) async-start(), calls=%async_computation.1 | async-start | bytes 6193152 | tf_op jit(solution)/shard_map/psum | solution.py:30
  13.9 9.1 %collective-permute-start.1 = (f32[8,1,128]{2,1,0:T(1,128)S(1)}, f32[8,1,128]{2,1,0:T(1,128)S(1)}, u32[]{:S(2)}, u32[]{:S(2)}) collective-permute-start(f32[8,1,128]{2,1,0:T(1,128)S(1)} %get-tuple-element.182), channel_id=1, source_target_pairs={{0,8},{8,16},{16,24},{24,32},{32,40},{40,48},{48,56},{1,9},{9,17},... | collective-permute-start | bytes 12296 | tf_op jit(solution)/shard_map/ppermute | solution.py:22
  18.1 5.0 collective-permute-start
  23.2 8.0 collective-permute-start.3
  28.5 5.9 collective-permute-start.2
  34.7 5.7 collective-permute-start.4
  36.0 5.2 collective-permute-start.5
  41.3 5.5 collective-permute-start.7
  44.0 7.8 collective-permute-start.6
  52.0 5.0 collective-permute-start.9
  55.7 6.3 collective-permute-start.8
  64.6 5.9 collective-permute-start.10
  70.8 6.4 collective-permute-start.12
  72.1 5.8 collective-permute-start.13
  78.1 5.3 collective-permute-start.15
  80.8 7.3 collective-permute-start.14
  88.3 7.7 collective-permute-start.17
  94.7 5.2 collective-permute-start.16
  102.2 6.4 collective-permute-start.18
  108.8 6.3 collective-permute-start.20
  110.1 5.7 collective-permute-start.21
  115.9 5.5 collective-permute-start.23
  118.6 9.0 %collective-permute-start.22 = (f32[2,8,18,1]{3,2,1,0:T(8,128)S(1)}, f32[2,8,18,1]{3,2,1,0:T(8,128)S(1)}, u32[]{:S(2)}, u32[]{:S(2)}) collective-permute-start(f32[2,8,18,1]{3,2,1,0:T(8,128)S(1)} %get-tuple-element.35), channel_id=1, source_target_pairs={{1,0},{2,1},{3,2},{4,3},{5,4},{6,5},{7,6},{9,8},{10,9},{11,10},{12... | collective-permute-start | bytes 3464 | tf_op jit(solution)/shard_map/ppermute | solution.py:23
  127.8 445.8 %collective-permute-start.25 = (f32[8,1,128]{2,1,0:T(1,128)S(1)}, f32[8,1,128]{2,1,0:T(1,128)S(1)}, u32[]{:S(2)}, u32[]{:S(2)}) collective-permute-start(f32[8,1,128]{2,1,0:T(1,128)S(1)} %get-tuple-element.171), channel_id=1, source_target_pairs={{0,8},{8,16},{16,24},{24,32},{32,40},{40,48},{48,56},{1,9},{9,17},... | collective-permute-start | bytes 12296 | tf_op jit(solution)/shard_map/ppermute | solution.py:22
  132.1 441.5 %collective-permute-start.24 = (f32[8,1,128]{2,1,0:T(1,128)S(1)}, f32[8,1,128]{2,1,0:T(1,128)S(1)}, u32[]{:S(2)}, u32[]{:S(2)}) collective-permute-start(f32[8,1,128]{2,1,0:T(1,128)S(1)} %get-tuple-element.172), channel_id=1, source_target_pairs={{8,0},{16,8},{24,16},{32,24},{40,32},{48,40},{56,48},{9,1},{17,9},... | collective-permute-start | bytes 12296 | tf_op jit(solution)/shard_map/ppermute | solution.py:23
  573.7 5.7 collective-permute-start.27
  575.6 5.9 collective-permute-start.26
  581.7 5.3 collective-permute-start.28
  583.0 4.8 collective-permute-start.29
  588.0 10.5 %collective-permute-start.31 = (f32[2,8,18,1]{3,2,1,0:T(8,128)S(1)}, f32[2,8,18,1]{3,2,1,0:T(8,128)S(1)}, u32[]{:S(2)}, u32[]{:S(2)}) collective-permute-start(f32[2,8,18,1]{3,2,1,0:T(8,128)S(1)} %get-tuple-element.34), channel_id=1, source_target_pairs={{0,1},{1,2},{2,3},{3,4},{4,5},{5,6},{6,7},{8,9},{9,10},{10,11},{11... | collective-permute-start | bytes 3464 | tf_op jit(solution)/shard_map/ppermute | solution.py:22
  590.9 69.9 %collective-permute-start.30 = (f32[2,8,18,1]{3,2,1,0:T(8,128)S(1)}, f32[2,8,18,1]{3,2,1,0:T(8,128)S(1)}, u32[]{:S(2)}, u32[]{:S(2)}) collective-permute-start(f32[2,8,18,1]{3,2,1,0:T(8,128)S(1)} %get-tuple-element.33), channel_id=1, source_target_pairs={{1,0},{2,1},{3,2},{4,3},{5,4},{6,5},{7,6},{9,8},{10,9},{11,10},{12... | collective-permute-start | bytes 3464 | tf_op jit(solution)/shard_map/ppermute | solution.py:23
  (5 other events, 26.2 us)
Sparse Core Ops, SparseCore 0:
  14.0 557.5 all-reduce.2
  574.5 279.5 all-reduce.4
where the time goes:
time: 867 us; the launch traced here: 866 us
  waiting for transfers between devices  743 us (86%)
  starting transfers between devices  88.2 us (10%)
  between operations  14.5 us (2%)
  other arithmetic  10.4 us (1%)
    psum x1, waiting for transfers between devices, local(): summed = lax.psum(pieces, ('gx', 'gy'))  438 us
    psum x1, waiting for transfers between devices, broadcast(): return lax.psum(block, axis)  193 us
    ppermute x16, waiting for transfers between devices, extended(): after = lax.ppermute(initial, axis, down)  100 us
    ppermute x16, starting transfers between devices, extended(): before = lax.ppermute(last, axis, up)  59.8 us
    ppermute x16, starting transfers between devices, extended(): after = lax.ppermute(initial, axis, down)  28.4 us
  transfers between devices with their start and end apart: 34, of which 20 were waited for; matrix products, arithmetic and copies ran while one was open for 1% of the time, Pallas kernels for 0%

commit v1 on v0

--- a/solution.py
+++ b/solution.py
@@ -10,6 +10,7 @@
 TIME_STEP = 0.5
 SOUND_SQ = 1.0
 PRECISE = lax.Precision.HIGHEST
+shape_strings = lambda frame, bus_axis: lax.all_gather(frame, bus_axis).sum(axis=0)
 
 
 def extended(value, sides, width):
@@ -27,7 +28,7 @@
 
 def broadcast(block, axis, owner):
     block = jnp.where(lax.axis_index(axis) == owner, block, jnp.zeros_like(block))
-    return lax.psum(block, axis)
+    return shape_strings(block, axis)
 
 
 def vertical(field):

time: 867 us -> 1050 us (1.21)
  waiting for transfers between devices: 743 us -> 915 us
    all_gather x0 -> x1, waiting for transfers between devices: none -> 221 us  [lax.all_gather(frame, bus_axis).sum(axis=0)]
    psum x1 -> x0, waiting for transfers between devices: 193 us -> none  [broadcast(): return lax.psum(block, axis)]
    psum x1, waiting for transfers between devices: 438 us -> 557 us  [local(): summed = lax.psum(pieces, ('gx', 'gy'))]
    ppermute x16, waiting for transfers between devices: 11 us -> 30.3 us  [extended(): before = lax.ppermute(last, axis, up)]
  transfers between devices with their start and end apart: 34 -> 34, of which waited for: 20 -> 23; matrix products, arithmetic and copies ran while one was open for 1% -> 1% of each run, Pallas kernels for 0% -> 0%
where the time goes in v1:
time: 1050 us; the launch traced here: 1040 us
  waiting for transfers between devices  915 us (87%)
  starting transfers between devices  87 us (8%)
  other arithmetic  19.6 us (2%)
  between operations  14.5 us (1%)
    psum x1, waiting for transfers between devices, local(): summed = lax.psum(pieces, ('gx', 'gy'))  557 us
    all_gather x1, waiting for transfers between devices, lax.all_gather(frame, bus_axis).sum(axis=0)  221 us
    ppermute x16, waiting for transfers between devices, extended(): after = lax.ppermute(initial, axis, down)  106 us
    ppermute x16, starting transfers between devices, extended(): before = lax.ppermute(last, axis, up)  57 us
    ppermute x16, waiting for transfers between devices, extended(): before = lax.ppermute(last, axis, up)  30.3 us
    ppermute x16, starting transfers between devices, extended(): after = lax.ppermute(initial, axis, down)  30 us
  transfers between devices with their start and end apart: 34, of which 23 were waited for; matrix products, arithmetic and copies ran while one was open for 1% of the time, Pallas kernels for 0%

profile of v1, /device:TPU:1, one launch (start us, length us, event | category | flops | bytes accessed | tf_op | source)
XLA Modules:
  0.0 1044.3 jit_solution(14581259869398359712)
XLA Ops:
  13.9 557.2 %all-reduce.2.cloned.1.call-done = f32[7,4,3,8,3,384]{5,3,4,2,1,0:T(8,128)} async-done(((f32[7,4,3,8,3,384]{5,3,4,2,1,0:T(8,128)}), f32[7,4,3,8,3,384]{5,3,4,2,1,0:T(8,128)}) %all-reduce.2.cloned.1.call-update) | async-done | bytes 3096592 | tf_op jit(solution)/shard_map/psum | solution.py:154
  581.3 4.4 collective-permute-start.2
  588.7 4.6 collective-permute-start.5
  594.3 2.7 collective-permute-start.7
  598.9 7.5 collective-permute-done.7
  606.4 8.6 collective-permute-done.6
  615.2 4.7 collective-permute-start.9
  621.2 5.3 collective-permute-done.8
  628.6 2.4 collective-permute-start.10
  632.5 15.6 %collective-permute-done.10 = f32[8,18,1]{2,1,0:T(8,128)S(1)} collective-permute-done((f32[8,18,1]{2,1,0:T(8,128)S(1)}, f32[8,18,1]{2,1,0:T(8,128)S(1)}, u32[]{:S(2)}, u32[]{:S(2)}) %collective-permute-start.10) | collective-permute-done | bytes 608 | tf_op jit(solution)/shard_map/ppermute | solution.py:24
  649.7 12.7 %collective-permute-start.13 = (f32[2,8,1,128]{3,2,1,0:T(1,128)S(1)}, f32[2,8,1,128]{3,2,1,0:T(1,128)S(1)}, u32[]{:S(2)}, u32[]{:S(2)}) collective-permute-start(f32[2,8,1,128]{3,2,1,0:T(1,128)S(1)} %get-tuple-element.47), channel_id=1, source_target_pairs={{0,8},{8,16},{16,24},{24,32},{32,40},{40,48},{48,56},{1,9},{9,17},... | collective-permute-start | bytes 24584 | tf_op jit(solution)/shard_map/ppermute | solution.py:23
  665.2 2.4 collective-permute-start.14
  667.7 4.5 collective-permute-done.15
  672.1 8.9 collective-permute-done.14
  681.2 4.0 collective-permute-start.17
  686.6 3.0 collective-permute-done.16
  689.7 2.8 collective-permute-start.19
  694.6 3.9 collective-permute-done.18
  699.9 4.0 collective-permute-start.21
  704.8 3.0 collective-permute-start.23
  709.7 6.6 collective-permute-done.23
  716.4 6.4 collective-permute-done.22
  723.0 3.4 collective-permute-start.25
  727.8 4.0 collective-permute-done.24
  733.8 2.4 collective-permute-start.26
  738.4 30.2 %collective-permute-done.26 = f32[8,18,1]{2,1,0:T(8,128)S(1)} collective-permute-done((f32[8,18,1]{2,1,0:T(8,128)S(1)}, f32[8,18,1]{2,1,0:T(8,128)S(1)}, u32[]{:S(2)}, u32[]{:S(2)}) %collective-permute-start.26) | collective-permute-done | bytes 608 | tf_op jit(solution)/shard_map/ppermute | solution.py:24
  770.0 4.0 collective-permute-start.29
  777.1 2.2 collective-permute-start.30
  779.3 5.3 collective-permute-done.31
  784.6 19.2 %collective-permute-done.30 = f32[2,8,18,1]{3,2,1,0:T(8,128)S(1)} collective-permute-done((f32[2,8,18,1]{3,2,1,0:T(8,128)S(1)}, f32[2,8,18,1]{3,2,1,0:T(8,128)S(1)}, u32[]{:S(2)}, u32[]{:S(2)}) %collective-permute-start.30) | collective-permute-done | bytes 1184 | tf_op jit(solution)/shard_map/ppermute | solution.py:24
  804.1 221.3 %all-gather.3.cloned.1.call-done = f32[56,4,3,8,3,384]{5,3,4,2,1,0:T(8,128)} async-done(((f32[7,4,3,8,3,384]{5,3,4,2,1,0:T(8,128)}), f32[56,4,3,8,3,384]{5,3,4,2,1,0:T(8,128)}) %all-gather.3.cloned.1.call-update) | async-done | bytes 24772624 | tf_op jit(solution)/shard_map/all_gather | solution.py:13
  1025.4 9.3 reduce_sum.9
  (160 shorter events, 53.4 us)
Async XLA Ops:
  6.5 564.5 %all-reduce.2.cloned.1.call-start = ((), (), s32[]{:S(2)}) async-start(), calls=%async_computation | async-start | bytes 6193152 | tf_op jit(solution)/shard_map/psum | solution.py:154
  13.8 1011.6 %all-gather.3.cloned.1.call-start = ((), (), s32[]{:S(2)}) async-start(), calls=%async_computation.1 | async-start | bytes 27869184 | tf_op jit(solution)/shard_map/all_gather | solution.py:13
  573.0 6.2 collective-permute-start.1
  574.4 4.8 collective-permute-start
  579.4 6.5 collective-permute-start.3
  581.3 5.9 collective-permute-start.2
  587.4 6.0 collective-permute-start.4
  588.7 5.4 collective-permute-start.5
  594.3 12.1 %collective-permute-start.7 = (f32[2,8,18,1]{3,2,1,0:T(8,128)S(1)}, f32[2,8,18,1]{3,2,1,0:T(8,128)S(1)}, u32[]{:S(2)}, u32[]{:S(2)}) collective-permute-start(f32[2,8,18,1]{3,2,1,0:T(8,128)S(1)} %get-tuple-element.40), channel_id=1, source_target_pairs={{0,1},{1,2},{2,3},{3,4},{4,5},{5,6},{6,7},{8,9},{9,10},{10,11},{11... | collective-permute-start | bytes 3464 | tf_op jit(solution)/shard_map/ppermute | solution.py:23
  596.9 18.1 %collective-permute-start.6 = (f32[2,8,18,1]{3,2,1,0:T(8,128)S(1)}, f32[2,8,18,1]{3,2,1,0:T(8,128)S(1)}, u32[]{:S(2)}, u32[]{:S(2)}) collective-permute-start(f32[2,8,18,1]{3,2,1,0:T(8,128)S(1)} %get-tuple-element.39), channel_id=1, source_target_pairs={{1,0},{2,1},{3,2},{4,3},{5,4},{6,5},{7,6},{9,8},{10,9},{11,10},{12... | collective-permute-start | bytes 3464 | tf_op jit(solution)/shard_map/ppermute | solution.py:24
  615.2 6.0 collective-permute-start.9
  619.9 6.6 collective-permute-start.8
  626.6 5.9 collective-permute-start.11
  628.6 19.6 %collective-permute-start.10 = (f32[8,18,1]{2,1,0:T(8,128)S(1)}, f32[8,18,1]{2,1,0:T(8,128)S(1)}, u32[]{:S(2)}, u32[]{:S(2)}) collective-permute-start(f32[8,18,1]{2,1,0:T(8,128)S(1)} %get-tuple-element.55), channel_id=1, source_target_pairs={{1,0},{2,1},{3,2},{4,3},{5,4},{6,5},{7,6},{9,8},{10,9},{11,10},{12... | collective-permute-start | bytes 1736 | tf_op jit(solution)/shard_map/ppermute | solution.py:24
  648.4 14.1 %collective-permute-start.12 = (f32[2,8,1,128]{3,2,1,0:T(1,128)S(1)}, f32[2,8,1,128]{3,2,1,0:T(1,128)S(1)}, u32[]{:S(2)}, u32[]{:S(2)}) collective-permute-start(f32[2,8,1,128]{3,2,1,0:T(1,128)S(1)} %get-tuple-element.48), channel_id=1, source_target_pairs={{8,0},{16,8},{24,16},{32,24},{40,32},{48,40},{56,48},{9,1},{17,9},... | collective-permute-start | bytes 24584 | tf_op jit(solution)/shard_map/ppermute | solution.py:24
  649.7 13.5 %collective-permute-start.13 = (f32[2,8,1,128]{3,2,1,0:T(1,128)S(1)}, f32[2,8,1,128]{3,2,1,0:T(1,128)S(1)}, u32[]{:S(2)}, u32[]{:S(2)}) collective-permute-start(f32[2,8,1,128]{3,2,1,0:T(1,128)S(1)} %get-tuple-element.47), channel_id=1, source_target_pairs={{0,8},{8,16},{16,24},{24,32},{32,40},{40,48},{48,56},{1,9},{9,17},... | collective-permute-start | bytes 24584 | tf_op jit(solution)/shard_map/ppermute | solution.py:23
  663.3 8.8 collective-permute-start.15
  665.2 15.8 %collective-permute-start.14 = (f32[2,8,18,1]{3,2,1,0:T(8,128)S(1)}, f32[2,8,18,1]{3,2,1,0:T(8,128)S(1)}, u32[]{:S(2)}, u32[]{:S(2)}) collective-permute-start(f32[2,8,18,1]{3,2,1,0:T(8,128)S(1)} %get-tuple-element.37), channel_id=1, source_target_pairs={{1,0},{2,1},{3,2},{4,3},{5,4},{6,5},{7,6},{9,8},{10,9},{11,10},{12... | collective-permute-start | bytes 3464 | tf_op jit(solution)/shard_map/ppermute | solution.py:24
  681.2 5.4 collective-permute-start.17
  689.7 4.8 collective-permute-start.19
  692.5 5.9 collective-permute-start.18
  698.6 5.4 collective-permute-start.20
  704.8 11.5 %collective-permute-start.23 = (f32[2,8,18,1]{3,2,1,0:T(8,128)S(1)}, f32[2,8,18,1]{3,2,1,0:T(8,128)S(1)}, u32[]{:S(2)}, u32[]{:S(2)}) collective-permute-start(f32[2,8,18,1]{3,2,1,0:T(8,128)S(1)} %get-tuple-element.36), channel_id=1, source_target_pairs={{0,1},{1,2},{2,3},{3,4},{4,5},{5,6},{6,7},{8,9},{9,10},{10,11},{11... | collective-permute-start | bytes 3464 | tf_op jit(solution)/shard_map/ppermute | solution.py:23
  707.8 15.0 %collective-permute-start.22 = (f32[2,8,18,1]{3,2,1,0:T(8,128)S(1)}, f32[2,8,18,1]{3,2,1,0:T(8,128)S(1)}, u32[]{:S(2)}, u32[]{:S(2)}) collective-permute-start(f32[2,8,18,1]{3,2,1,0:T(8,128)S(1)} %get-tuple-element.35), channel_id=1, source_target_pairs={{1,0},{2,1},{3,2},{4,3},{5,4},{6,5},{7,6},{9,8},{10,9},{11,10},{12... | collective-permute-start | bytes 3464 | tf_op jit(solution)/shard_map/ppermute | solution.py:24
  723.0 4.8 collective-permute-start.25
  726.4 5.4 collective-permute-start.24
  731.9 6.5 collective-permute-start.27
  733.8 34.7 %collective-permute-start.26 = (f32[8,18,1]{2,1,0:T(8,128)S(1)}, f32[8,18,1]{2,1,0:T(8,128)S(1)}, u32[]{:S(2)}, u32[]{:S(2)}) collective-permute-start(f32[8,18,1]{2,1,0:T(8,128)S(1)} %get-tuple-element.51), channel_id=1, source_target_pairs={{1,0},{2,1},{3,2},{4,3},{5,4},{6,5},{7,6},{9,8},{10,9},{11,10},{12... | collective-permute-start | bytes 1736 | tf_op jit(solution)/shard_map/ppermute | solution.py:24
  768.7 5.4 collective-permute-start.28
  770.0 4.8 collective-permute-start.29
  775.0 9.7 collective-permute-start.31
  777.1 26.7 %collective-permute-start.30 = (f32[2,8,18,1]{3,2,1,0:T(8,128)S(1)}, f32[2,8,18,1]{3,2,1,0:T(8,128)S(1)}, u32[]{:S(2)}, u32[]{:S(2)}) collective-permute-start(f32[2,8,18,1]{3,2,1,0:T(8,128)S(1)} %get-tuple-element.33), channel_id=1, source_target_pairs={{1,0},{2,1},{3,2},{4,3},{5,4},{6,5},{7,6},{9,8},{10,9},{11,10},{12... | collective-permute-start | bytes 3464 | tf_op jit(solution)/shard_map/ppermute | solution.py:24
  (5 other events, 24.4 us)
Sparse Core Ops, SparseCore 0:
  14.0 557.0 all-reduce.1
  574.3 451.0 all-gather.2
